TPU v7x, 32 devices: a whole 2x2x4 slice. The times are simulated.
32 devices in a mesh: grp: 2 (over y), row: 8 (over z, core), col: 2 (over x).
Axes of the slice: x: 2, y: 2, z: 4, core: 2. Of those that a mesh axis runs over, the one named last changes fastest.
Arguments:
- pair: bfloat16 [192, 96, 128], P(('grp', 'row'), 'col'), parts along dimension 0, may hold values from -6 to 6
- token_count: int32 [2], P('grp'), parts along dimension 0, may hold values from 72 to 96
- tri_in: bfloat16 [2, 128, 512], replicated, may hold values from -0.5 to 0.5
- tri_gate: bfloat16 [2, 128, 128], replicated, may hold values from -0.5 to 0.5
- tri_out: bfloat16 [2, 128, 128], replicated, may hold values from -0.5 to 0.5
- trans_in: bfloat16 [128, 1024], replicated, may hold values from -0.5 to 0.5
- trans_out: bfloat16 [512, 128], replicated, may hold values from -0.25 to 0.25
Outputs:
- pair_out: bfloat16 [192, 96, 128], P(('grp', 'row'), 'col'), parts along dimension 0
There are 2 independent parts, one for each index of `grp`. A program takes and returns all parts, laid end to end along the dimension named above; an argument that names none is the same for every part. Nothing has to cross between parts.
Inputs may be any that keep to these rules, and one draw needn't show every extreme that they name: `token_count`: the number of real tokens of the complex; pair entries with either token index at or past it are padding.
All inputs are finite; a program needn't handle non-finite values.
Results may differ from a plain program's by a relative error of at most 0.015.
Values may be sent and summed in bfloat16 or wider, within the bound.
No kernel may reach another device: no remote copies, remote signals or barrier semaphores. Data moves between devices by JAX's collectives and lax.ppermute only.
A program may use at most 64 MiB of HBM per device.

v0:
```python
import jax
import jax.numpy as jnp
from jax import lax
from jax.sharding import PartitionSpec as P


def layer_norm(values, along):
    average = jnp.mean(values, axis=along, keepdims=True)
    centred = values - average
    spread = jnp.mean(centred * centred, axis=along, keepdims=True)
    return centred * lax.rsqrt(spread + 1e-05)


def contract_rows(left_side, right_side):
    return jnp.einsum("hik,hjk->hij", left_side, right_side, preferred_element_type=jnp.float32)


def contract_columns(left_side, right_side):
    return jnp.einsum("hki,hkj->hij", left_side, right_side, preferred_element_type=jnp.float32)


def body(pair, token_count, tri_in, tri_gate, tri_out, trans_in, trans_out):
    tile_rows, tile_cols, pair_width = pair.shape
    hidden = tri_out.shape[1]
    ffn_width = trans_out.shape[0]
    row_place = lax.axis_index("row")
    col_place = lax.axis_index("col")
    row_first = row_place * tile_rows
    col_first = col_place * tile_cols
    token_limit = token_count[0]
    row_keep = (row_first + jnp.arange(tile_rows, dtype=jnp.int32) < token_limit).astype(
        jnp.float32
    )
    col_keep = (col_first + jnp.arange(tile_cols, dtype=jnp.int32) < token_limit).astype(
        jnp.float32
    )
    keep_mask = row_keep[:, None] * col_keep[None, :]

    def project(stream, which_side):
        normed = layer_norm(stream.astype(jnp.float32), 2).astype(jnp.bfloat16)
        weight = tri_in[which_side].reshape(pair_width, 4, hidden)
        projected = jnp.einsum("ijc,cgh->ghij", normed, weight, preferred_element_type=jnp.float32)
        left_side = (keep_mask * jax.nn.sigmoid(projected[2]) * projected[0]).astype(jnp.bfloat16)
        right_side = (keep_mask * jax.nn.sigmoid(projected[3]) * projected[1]).astype(jnp.bfloat16)
        gate_value = jax.nn.sigmoid(
            jnp.dot(normed, tri_gate[which_side], preferred_element_type=jnp.float32)
        )
        return (left_side, right_side, gate_value)

    def finish(stream, mixed_sum, gate_value, which_side):
        normed = layer_norm(mixed_sum, 0).astype(jnp.bfloat16)
        update = gate_value * jnp.einsum(
            "hij,hc->ijc", normed, tri_out[which_side], preferred_element_type=jnp.float32
        )
        return (stream.astype(jnp.float32) + keep_mask[:, :, None] * update).astype(jnp.bfloat16)

    left_side, right_side, gate_value = project(pair, 0)
    partial_rows = contract_rows(left_side, lax.all_gather(right_side, "row", axis=1, tiled=True))
    mixed_sum = lax.psum_scatter(partial_rows, "col", scatter_dimension=2, tiled=True)
    stream = finish(pair, mixed_sum, gate_value, 0)
    left_side, right_side, gate_value = project(stream, 1)
    left_rows = lax.all_gather(left_side, "col", axis=2, tiled=True)
    column_strip = lax.all_to_all(left_rows, "row", split_axis=2, concat_axis=1, tiled=True)
    mixed_sum = contract_columns(
        column_strip, lax.all_gather(right_side, "row", axis=1, tiled=True)
    )
    stream = finish(stream, mixed_sum, gate_value, 1)
    normed = layer_norm(stream.astype(jnp.float32), 2).astype(jnp.bfloat16)
    inner_sum = jnp.dot(normed, trans_in, preferred_element_type=jnp.float32)
    activation = (jax.nn.silu(inner_sum[..., :ffn_width]) * inner_sum[..., ffn_width:]).astype(
        jnp.bfloat16
    )
    update = jnp.dot(activation, trans_out, preferred_element_type=jnp.float32)
    return (stream.astype(jnp.float32) + keep_mask[:, :, None] * update).astype(jnp.bfloat16)


def solution(mesh):
    placed = (P(("grp", "row"), "col", None), P("grp"), P(), P(), P(), P(), P())
    return jax.shard_map(
        body, mesh=mesh, in_specs=placed, out_specs=P(("grp", "row"), "col", None), check_vma=False
    )
```

profile of v0, /device:TPU:0, one launch (start us, length us, event | category | flops | bytes accessed | tf_op | source)
XLA Modules:
  0.0 121.3 jit_solution(946812768014044533)
XLA Ops:
  7.2 1.1 convert_reduce_fusion
  8.3 1.2 fusion.21
  9.5 1.6 %fusion.72 = (bf16[1,128,512]{2,1,0:T(8,128)(2,1)}, bf16[1,128,512]{2,1,0:T(8,128)(2,1)S(1)}) fusion(bf16[2,128,512]{2,1,0:T(8,128)(2,1)} %param.9), kind=kLoop, calls=%fused_computation.108 | loop fusion | bytes 524288 | tf_op jit(solution)/shard_map/slice | solution.py:41
  11.2 0.1 copy.110
  11.3 0.1 broadcast_multiply_fusion.5
  11.4 0.4 convolution_bitcast_fusion.1
  11.8 0.9 fusion.38
  12.7 0.0 all-gather.3.cloned.1.call-update
  12.7 0.0 reduce-scatter.2.cloned.1.call-start
  12.7 1.2 %copy.84 = bf16[128,12,48]{2,1,0:T(8,128)(2,1)} copy(bf16[128,12,48]{0,2,1:T(8,128)(2,1)S(1)} %get-tuple-element.8) | data formatting | bytes 294912 | tf_op jit(solution)/shard_map/convert_element_type | solution.py:43
  14.0 24.4 %all-gather.3.cloned.1.call-done = bf16[128,96,48]{0,2,1:T(8,128)(2,1)} async-done(((bf16[128,12,48]{0,2,1:T(8,128)(2,1)}), bf16[128,96,48]{0,2,1:T(8,128)(2,1)}) %all-gather.3.cloned.1.call-update) | async-done | bytes 1179664 | tf_op jit(solution)/shard_map/all_gather | solution.py:58
  38.3 5.3 %copy.85 = bf16[128,96,48]{2,1,0:T(8,128)(2,1)S(1)} copy(bf16[128,96,48]{0,2,1:T(8,128)(2,1)} %all-gather.3.cloned.1.call-done) | data formatting | bytes 2359296 | tf_op jit(solution)/shard_map/all_gather | solution.py:58
  43.6 3.7 %fusion.76 = f32[128,12,96]{2,1,0:T(8,128)} fusion(bf16[128,12,48]{2,1,0:T(8,128)(2,1)} %copy.84, bf16[128,96,48]{2,1,0:T(8,128)(2,1)S(1)} %copy.85), kind=kOutput, calls=%fused_computation.112 | convolution fusion | flops 14155776 | bytes 1916928 | tf_op jit(solution)/shard_map/hik,hjk->hij/dot_general | solution.py:15
  47.4 2.7 %copy.86 = f32[128,12,96]{0,1,2:T(8,128)} copy(f32[128,12,96]{2,1,0:T(8,128)} %fusion.76) | data formatting | bytes 1179648 | tf_op jit(solution)/shard_map/hik,hjk->hij/dot_general | solution.py:15
  50.1 0.0 reduce-scatter.2.cloned.1.call-update
  50.2 0.0 all-gather.5.cloned.1.call-start
  50.2 0.1 copy.114
  50.4 0.3 fusion.11
  50.7 16.7 %reduce-scatter.2.cloned.1.call-done = f32[128,12,48]{0,1,2:T(8,128)} async-done(((f32[128,12,96]{0,1,2:T(8,128)}), f32[128,12,48]{0,1,2:T(8,128)}) %reduce-scatter.2.cloned.1.call-update) | async-done | bytes 294928 | tf_op jit(solution)/shard_map/reduce_scatter | solution.py:59
  67.5 1.2 %reduce_sum.92 = f32[12,48]{0,1:T(8,128)S(1)} reduce(f32[128,12,48]{0,1,2:T(8,128)} %reduce-scatter.2.cloned.1.call-done, f32[]{:T(128)} %constant.32.clone.1), dimensions={0}, to_apply=%region_3.0 | reduce | flops 73152 | bytes 297220 | tf_op jit(solution)/shard_map/reduce_sum | solution.py:8
  68.7 0.1 copy.87
  68.8 0.1 copy.88
  68.9 1.3 %multiply_reduce_fusion.1 = f32[12,48]{0,1:T(8,128)S(1)} fusion(f32[128,12,48]{0,1,2:T(8,128)} %reduce-scatter.2.cloned.1.call-done, f32[12,48]{0,1:T(8,128)S(1)} %copy.88), kind=kLoop, calls=%fused_computation.31 | loop fusion | flops 220608 | bytes 299520 | tf_op jit(solution)/shard_map/reduce_sum | solution.py:10
  70.2 0.1 copy.89
  70.3 0.1 copy.90
  70.4 0.3 multiply_convert_fusion.1
  70.7 0.3 fusion.73
  71.0 0.3 multiply_reduce_fusion.3
  71.3 0.4 convolution_bitcast_fusion
  71.7 0.9 fusion.24
  72.6 6.1 %all_gather.10 = bf16[128,12,96]{0,2,1:T(8,128)(2,1)S(1)} all-gather(bf16[128,12,48]{0,2,1:T(8,128)(2,1)S(1)} %get-tuple-element.6), channel_id=1, replica_groups=mesh['grp'=2,'row'=8,'col'=2] {'col'}, dimensions={2}, use_global_device_ids=true | all-gather | bytes 442368 | tf_op jit(solution)/shard_map/all_gather | solution.py:62
  78.6 0.9 copy.95
  79.5 4.6 %all-to-all-start = ((bf16[128,12,96]{0,1,2:T(8,128)(2,1)}), bf16[128,12,96]{0,1,2:T(8,128)(2,1)S(1)}, u32[]{:S(2)}, u32[]{:S(2)}) async-start(bf16[128,12,96]{0,1,2:T(8,128)(2,1)} %copy.95), calls=%async_computation.1 | async-start | bytes 786432 | tf_op jit(solution)/shard_map/all_to_all | solution.py:63
  84.1 1.1 fusion.8
  85.2 17.1 %all-to-all-done = bf16[128,12,96]{0,1,2:T(8,128)(2,1)S(1)} async-done(((bf16[128,12,96]{0,1,2:T(8,128)(2,1)}), bf16[128,12,96]{0,1,2:T(8,128)(2,1)S(1)}, u32[]{:S(2)}, u32[]{:S(2)}) %all-to-all-start) | async-done | bytes 294944 | tf_op jit(solution)/shard_map/all_to_all | solution.py:63
  102.3 0.1 all_to_all.16
  102.4 1.2 %copy.98 = bf16[128,96,12]{1,2,0:T(8,128)(2,1)} copy(bf16[128,96,12]{0,1,2:T(8,128)(2,1)S(1)} %all_to_all.16) | data formatting | bytes 589824 | tf_op jit(solution)/shard_map/all_to_all | solution.py:63
  103.7 5.3 %copy.99 = bf16[128,96,48]{2,1,0:T(8,128)(2,1)S(1)} copy(bf16[128,96,48]{0,2,1:T(8,128)(2,1)} %all-gather.5.cloned.1.call-done) | data formatting | bytes 2359296 | tf_op jit(solution)/shard_map/all_gather | solution.py:65
  109.0 2.0 %fusion.74 = (f32[12,48]{1,0:T(8,128)S(1)}, f32[128,12,48]{2,1,0:T(8,128)S(1)}) fusion(bf16[128,96,12]{1,2,0:T(8,128)(2,1)} %copy.98, bf16[128,96,48]{2,1,0:T(8,128)(2,1)S(1)} %copy.99), kind=kOutput, calls=%fused_computation.110 | convolution fusion | flops 14228928 | bytes 1771776 | tf_op jit(solution)/shard_map/hki,hkj->hij/dot_general | solution.py:19
  111.0 0.2 multiply_reduce_fusion
  111.2 0.1 multiply_convert_fusion
  111.3 0.6 copy-done.2
  111.9 0.1 copy-done.6
  112.0 0.4 fusion.75
  112.4 0.3 multiply_reduce_fusion.2
  112.7 0.5 fusion.53
  113.3 0.4 copy-done.16
  113.6 1.1 fusion.14
  (49 shorter events, 0.2 us)
Async XLA Ops:
  6.5 106.2 %copy-start = (bf16[128,1024]{1,0:T(8,128)(2,1)S(1)}, bf16[128,1024]{1,0:T(8,128)(2,1)}, u32[]{:S(2)}) copy-start(bf16[128,1024]{1,0:T(8,128)(2,1)} %param.12) | copy-start | bytes 786436
  6.5 4.9 %copy-start.4 = (bf16[12,48,128]{2,1,0:T(8,128)(2,1)S(1)}, bf16[12,48,128]{2,1,0:T(8,128)(2,1)}, u32[]{:S(2)}) copy-start(bf16[12,48,128]{2,1,0:T(8,128)(2,1)} %param.7) | copy-start | bytes 442372
  6.5 31.8 %all-gather.3.cloned.1.call-start = ((), (), s32[]{:S(2)}) async-start(), calls=%async_computation.2 | async-start | bytes 1327104 | tf_op jit(solution)/shard_map/all_gather | solution.py:58
  8.3 3.5 %copy-start.10 = (f32[12,48]{1,0:T(8,128)}, f32[12,48]{1,0:T(8,128)S(1)}, u32[]{:S(2)}) copy-start(f32[12,48]{1,0:T(8,128)S(1)} %broadcast_multiply_fusion.4) | copy-start | bytes 6916
  9.5 3.1 %copy-start.14 = (f32[12,48]{1,0:T(8,128)}, f32[12,48]{1,0:T(8,128)S(1)}, u32[]{:S(2)}) copy-start(f32[12,48]{1,0:T(8,128)S(1)} %add_rsqrt_fusion.4) | copy-start | bytes 6916
  11.4 1.2 %copy-start.7 = (f32[12,48]{1,0:T(8,128)}, f32[12,48]{1,0:T(8,128)S(1)}, u32[]{:S(2)}) copy-start(f32[12,48]{1,0:T(8,128)S(1)} %broadcast_multiply_fusion.5) | copy-start | bytes 6916
  12.7 54.8 %reduce-scatter.2.cloned.1.call-start = ((), (), s32[]{:S(2)}) async-start(), calls=%async_computation.3 | async-start | bytes 1179648 | tf_op jit(solution)/shard_map/reduce_scatter | solution.py:59
  47.4 2.8 %copy-start.5 = (bf16[1,128,512]{2,1,0:T(8,128)(2,1)S(1)}, bf16[1,128,512]{2,1,0:T(8,128)(2,1)}, u32[]{:S(2)}) copy-start(bf16[1,128,512]{2,1,0:T(8,128)(2,1)} %get-tuple-element.9) | copy-start | bytes 393220
  47.4 2.9 %copy-start.11 = (f32[12,48]{1,0:T(8,128)S(1)}, f32[12,48]{1,0:T(8,128)}, u32[]{:S(2)}) copy-start(f32[12,48]{1,0:T(8,128)} %copy-done.10) | copy-start | bytes 6916
  47.4 2.9 %copy-start.15 = (f32[12,48]{1,0:T(8,128)S(1)}, f32[12,48]{1,0:T(8,128)}, u32[]{:S(2)}) copy-start(f32[12,48]{1,0:T(8,128)} %copy-done.14) | copy-start | bytes 6916
  47.4 3.0 %copy-start.17 = (bf16[2,128,128]{2,1,0:T(8,128)(2,1)S(1)}, bf16[2,128,128]{2,1,0:T(8,128)(2,1)}, u32[]{:S(2)}) copy-start(bf16[2,128,128]{2,1,0:T(8,128)(2,1)} %param.10) | copy-start | bytes 196612
  50.2 53.5 %all-gather.5.cloned.1.call-start = ((), (), s32[]{:S(2)}) async-start(), calls=%async_computation.4 | async-start | bytes 1327104 | tf_op jit(solution)/shard_map/all_gather | solution.py:65
  50.7 19.9 %copy-start.8 = (f32[12,48]{1,0:T(8,128)S(1)}, f32[12,48]{1,0:T(8,128)}, u32[]{:S(2)}) copy-start(f32[12,48]{1,0:T(8,128)} %copy-done.7) | copy-start | bytes 6916
  50.7 19.9 %copy-start.12 = (bf16[2,128,128]{2,1,0:T(8,128)(2,1)S(1)}, bf16[2,128,128]{2,1,0:T(8,128)(2,1)}, u32[]{:S(2)}) copy-start(bf16[2,128,128]{2,1,0:T(8,128)(2,1)} %param.11) | copy-start | bytes 196612
  67.5 2.9 %copy-start.3 = (f32[128,12,48]{0,1,2:T(8,128)S(1)}, f32[128,12,48]{0,1,2:T(8,128)}, u32[]{:S(2)}) copy-start(f32[128,12,48]{0,1,2:T(8,128)} %reduce-scatter.2.cloned.1.call-done) | copy-start | bytes 884740
  71.0 13.1 %copy-start.1 = (f32[12,48,128]{2,1,0:T(8,128)}, f32[12,48,128]{2,1,0:T(8,128)S(1)}, u32[]{:S(2)}) copy-start(f32[12,48,128]{2,1,0:T(8,128)S(1)} %get-tuple-element.12) | copy-start | bytes 884740
  79.5 22.8 %all-to-all-start = ((bf16[128,12,96]{0,1,2:T(8,128)(2,1)}), bf16[128,12,96]{0,1,2:T(8,128)(2,1)S(1)}, u32[]{:S(2)}, u32[]{:S(2)}) async-start(bf16[128,12,96]{0,1,2:T(8,128)(2,1)} %copy.95), calls=%async_computation.1 | async-start | bytes 786432 | tf_op jit(solution)/shard_map/all_to_all | solution.py:63
  111.0 1.0 copy-start.2
  111.0 1.0 copy-start.6
  111.0 1.0 copy-start.9
  111.0 1.0 copy-start.13
  112.7 0.9 copy-start.16
Sparse Core Ops, SparseCore 0:
  12.8 25.4 all-gather.2
  50.3 17.1 reduce-scatter.1
  72.7 30.0 all-gather.4
where the time goes:
time: 122 us; the launch traced here: 121 us
  waiting for transfers between devices  58.2 us (48%)
  local copies, waits for them, and re-layouts  20.1 us (16%)
  between operations  14.2 us (12%)
  matrix products  10.2 us (8%)
  other arithmetic  7.78 us (6%)
  blocking collectives  6.08 us (5%)
  starting transfers between devices  4.69 us (4%)
    all_gather x2, waiting for transfers between devices, body(): lax.all_gather(right_side, 'row', axis=1, tiled=True)  24.4 us
    all_to_all x1, waiting for transfers between devices, body(): lax.all_to_all(left_rows, 'row', split_axis=2, concat_axis=1, tiled=True)  17.1 us
    reduce_scatter x1, waiting for transfers between devices, body(): lax.psum_scatter(partial_rows, 'col', scatter_dimension=2, tiled=True)  16.7 us
    all_gather x2, local copies, waits for them, and re-layouts, body(): lax.all_gather(right_side, 'row', axis=1, tiled=True)  10.6 us
    all_gather x1, blocking collectives, body(): left_rows = lax.all_gather(left_side, 'col', axis=2, tiled=True)  6.08 us
    all_to_all x1, starting transfers between devices, body(): lax.all_to_all(left_rows, 'row', split_axis=2, concat_axis=1, tiled=True)  4.6 us
    dot_general x1, matrix products, contract_rows(): jnp.einsum('hik,hjk->hij', left_side, right_side, preferred_element_type=...  3.75 us
    reduce_sum x5, other arithmetic, layer_norm(): spread = jnp.mean(centred * centred, axis=along, keepdims=True)  3.23 us
  transfers between devices with their start and end apart: 4, of which 3 were waited for; matrix products, arithmetic and copies ran while one was open for 4% of the time, Pallas kernels for 0%

commit v1 on v0

--- a/solution.py
+++ b/solution.py
@@ -2,6 +2,27 @@
 import jax.numpy as jnp
 from jax import lax
 from jax.sharding import PartitionSpec as P
+
+
+def gather_around(x, axis, dim):
+    length, here, span = (lax.axis_size(axis), lax.axis_index(axis), x.shape[dim])
+    upward = [(i, (i + 1) % length) for i in range(length)]
+    left = [(i, (i - 1) % length) for i in range(length)]
+    out = jnp.zeros((*x.shape[:dim], length * span, *x.shape[dim + 1 :]), x.dtype)
+    out = lax.dynamic_update_slice_in_dim(out, x, here * span, axis=dim)
+    from_left = from_right = x
+    halfway = length // 2
+    for hop in range(1, halfway + 1):
+        from_left = lax.ppermute(from_left, axis, upward)
+        out = lax.dynamic_update_slice_in_dim(
+            out, from_left, (here - hop) % length * span, axis=dim
+        )
+        if hop < length - halfway:
+            from_right = lax.ppermute(from_right, axis, left)
+            out = lax.dynamic_update_slice_in_dim(
+                out, from_right, (here + hop) % length * span, axis=dim
+            )
+    return out
 
 
 def layer_norm(values, along):
@@ -55,7 +76,7 @@
         return (stream.astype(jnp.float32) + keep_mask[:, :, None] * update).astype(jnp.bfloat16)
 
     left_side, right_side, gate_value = project(pair, 0)
-    partial_rows = contract_rows(left_side, lax.all_gather(right_side, "row", axis=1, tiled=True))
+    partial_rows = contract_rows(left_side, gather_around(right_side, "row", 1))
     mixed_sum = lax.psum_scatter(partial_rows, "col", scatter_dimension=2, tiled=True)
     stream = finish(pair, mixed_sum, gate_value, 0)
     left_side, right_side, gate_value = project(stream, 1)

time: 122 us -> 337 us (2.76)
  local copies, waits for them, and re-layouts: 20.1 us -> 235 us
  waiting for transfers between devices: 58.2 us -> 46.3 us
  starting transfers between devices: 4.69 us -> 16.5 us
    dynamic_update_slice x0 -> x8, local copies, waits for them, and re-layouts: none -> 208 us  [the longest x4 114 us: gather_around(): lax.dynamic_update_slice_in_dim(out, from_left, (here - hop) % length * s...]
    all_gather x2 -> x1, waiting for transfers between devices: 24.4 us -> 0.01 us  [body(): lax.all_gather(right_side, 'row', axis=1, tiled=True)]
    ppermute x0 -> x7, local copies, waits for them, and re-layouts: none -> 13.4 us  [the longest x4 7.63 us: gather_around(): from_left = lax.ppermute(from_left, axis, upward)]
    ppermute x0 -> x7, starting transfers between devices: none -> 11.9 us  [the longest x3 11.3 us: gather_around(): from_right = lax.ppermute(from_right, axis, left)]
    ppermute x0 -> x7, waiting for transfers between devices: none -> 10.1 us  [the longest x4 10.1 us: gather_around(): from_left = lax.ppermute(from_left, axis, upward)]
    all_gather x2 -> x1, local copies, waits for them, and re-layouts: 10.6 us -> 5.29 us  [body(): lax.all_gather(right_side, 'row', axis=1, tiled=True)]
  transfers between devices with their start and end apart: 4 -> 10, of which waited for: 3 -> 5; matrix products, arithmetic and copies ran while one was open for 4% -> 59% of each run, Pallas kernels for 0% -> 0%
where the time goes in v1:
time: 337 us; the launch traced here: 336 us
  local copies, waits for them, and re-layouts  235 us (70%)
  waiting for transfers between devices  46.3 us (14%)
  starting transfers between devices  16.5 us (5%)
  between operations  14.7 us (4%)
  matrix products  8.96 us (3%)
  other arithmetic  8.04 us (2%)
  blocking collectives  6.08 us (2%)
    dynamic_update_slice x4, local copies, waits for them, and re-layouts, gather_around(): lax.dynamic_update_slice_in_dim(out, from_left, (here - hop) % length * s...  114 us
    dynamic_update_slice x3, local copies, waits for them, and re-layouts, gather_around(): lax.dynamic_update_slice_in_dim(out, from_right, (here + hop) % length *...  85.2 us
    reduce_scatter x1, waiting for transfers between devices, body(): lax.psum_scatter(partial_rows, 'col', scatter_dimension=2, tiled=True)  19.1 us
    all_to_all x1, waiting for transfers between devices, body(): lax.all_to_all(left_rows, 'row', split_axis=2, concat_axis=1, tiled=True)  17.1 us
    ppermute x3, starting transfers between devices, gather_around(): from_right = lax.ppermute(from_right, axis, left)  11.3 us
    ppermute x4, waiting for transfers between devices, gather_around(): from_left = lax.ppermute(from_left, axis, upward)  10.1 us
    dynamic_update_slice x1, local copies, waits for them, and re-layouts, gather_around(): out = lax.dynamic_update_slice_in_dim(out, x, here * span, axis=dim)  9.28 us
    ppermute x4, local copies, waits for them, and re-layouts, gather_around(): from_left = lax.ppermute(from_left, axis, upward)  7.63 us
  transfers between devices with their start and end apart: 10, of which 5 were waited for; matrix products, arithmetic and copies ran while one was open for 59% of the time, Pallas kernels for 0%

profile of v1, /device:TPU:0, one launch (start us, length us, event | category | flops | bytes accessed | tf_op | source)
XLA Modules:
  0.0 336.0 jit_solution(18014788370209144609)
XLA Ops:
  7.2 1.1 convert_reduce_fusion
  8.3 1.2 fusion.21
  9.5 1.0 fusion.72
  10.7 1.3 convolution_bitcast_fusion.1
  12.2 0.5 collective-permute-start
  12.8 4.1 %collective-permute-start.1 = (bf16[128,12,48]{0,2,1:T(8,128)(2,1)S(1)}, bf16[128,12,48]{0,2,1:T(8,128)(2,1)S(1)}, u32[]{:S(2)}, u32[]{:S(2)}) collective-permute-start(bf16[128,12,48]{0,2,1:T(8,128)(2,1)S(1)} %get-tuple-element.7), channel_id=1, source_target_pairs={{0,14},{2,0},{4,2},{6,4},{8,6},{10,8},{12,10},{14,12},{1,15},{3,1}... | collective-permute-start | bytes 442376 | tf_op jit(solution)/shard_map/ppermute | solution.py:21
  16.9 2.9 collective-permute-done
  19.8 3.5 %collective-permute-start.3 = (bf16[128,12,48]{0,2,1:T(8,128)(2,1)S(1)}, bf16[128,12,48]{0,2,1:T(8,128)(2,1)}, u32[]{:S(2)}, u32[]{:S(2)}) collective-permute-start(bf16[128,12,48]{0,2,1:T(8,128)(2,1)S(1)} %collective-permute-done.1), channel_id=1, source_target_pairs={{0,14},{2,0},{4,2},{6,4},{8,6},{10,8},{12,10},{14,12},{1,15},{3,1}... | collective-permute-start | bytes 442376 | tf_op jit(solution)/shard_map/ppermute | solution.py:21
  23.3 3.7 %collective-permute-done.2 = bf16[128,12,48]{0,2,1:T(8,128)(2,1)S(1)} collective-permute-done((bf16[128,12,48]{0,2,1:T(8,128)(2,1)S(1)}, bf16[128,12,48]{0,2,1:T(8,128)(2,1)S(1)}, u32[]{:S(2)}, u32[]{:S(2)}) %collective-permute-start.2) | collective-permute-done | bytes 147488 | tf_op jit(solution)/shard_map/ppermute | solution.py:16
  27.0 3.7 %collective-permute-start.5 = (bf16[128,12,48]{0,2,1:T(8,128)(2,1)}, bf16[128,12,48]{0,2,1:T(8,128)(2,1)}, u32[]{:S(2)}, u32[]{:S(2)}) collective-permute-start(bf16[128,12,48]{0,2,1:T(8,128)(2,1)} %collective-permute-done.3), channel_id=1, source_target_pairs={{0,14},{2,0},{4,2},{6,4},{8,6},{10,8},{12,10},{14,12},{1,15},{3,1}... | collective-permute-start | bytes 442376 | tf_op jit(solution)/shard_map/ppermute | solution.py:21
  30.7 3.5 %collective-permute-done.4 = bf16[128,12,48]{0,2,1:T(8,128)(2,1)} collective-permute-done((bf16[128,12,48]{0,2,1:T(8,128)(2,1)S(1)}, bf16[128,12,48]{0,2,1:T(8,128)(2,1)}, u32[]{:S(2)}, u32[]{:S(2)}) %collective-permute-start.4) | collective-permute-done | bytes 147488 | tf_op jit(solution)/shard_map/ppermute | solution.py:16
  34.3 1.0 copy.112
  35.4 1.2 copy.120
  36.8 9.3 %dynamic_update_slice.24 = bf16[128,96,48]{1,2,0:T(8,128)(2,1)S(1)} dynamic-update-slice(bf16[128,96,48]{1,2,0:T(8,128)(2,1)S(1)} %broadcast_in_dim.2, bf16[128,12,48]{1,2,0:T(8,128)(2,1)S(1)} %copy.112, s32[]{:T(128)} %constant.81.clone.1, s32[]{:T(128)S(6)} %select_n.55, s32[]{:T(128)} %constant.81.clone.1) | dynamic-update-slice | bytes 294916 | tf_op jit(solution)/shard_map/dynamic_update_slice | solution.py:12
  46.1 1.9 copy.113
  48.0 28.4 %dynamic_update_slice.25 = bf16[128,96,48]{1,2,0:T(8,128)(2,1)S(1)} dynamic-update-slice(bf16[128,96,48]{1,2,0:T(8,128)(2,1)S(1)} %dynamic_update_slice.24, bf16[128,12,48]{1,2,0:T(8,128)(2,1)S(1)} %copy.113, s32[]{:T(128)} %constant.81.clone.1, s32[]{:T(128)S(6)} %select_n.57, s32[]{:T(128)} %constant.81.clone.1) | dynamic-update-slice | bytes 294916 | tf_op jit(solution)/shard_map/dynamic_update_slice | solution.py:17
  76.4 1.9 copy.114
  78.3 28.4 %dynamic_update_slice.26 = bf16[128,96,48]{1,2,0:T(8,128)(2,1)S(1)} dynamic-update-slice(bf16[128,96,48]{1,2,0:T(8,128)(2,1)S(1)} %dynamic_update_slice.25, bf16[128,12,48]{1,2,0:T(8,128)(2,1)S(1)} %copy.114, s32[]{:T(128)} %constant.81.clone.1, s32[]{:T(128)S(6)} %select_n.59, s32[]{:T(128)} %constant.81.clone.1) | dynamic-update-slice | bytes 294916 | tf_op jit(solution)/shard_map/dynamic_update_slice | solution.py:22
  106.7 1.9 copy.115
  108.7 28.4 %dynamic_update_slice.27 = bf16[128,96,48]{1,2,0:T(8,128)(2,1)S(1)} dynamic-update-slice(bf16[128,96,48]{1,2,0:T(8,128)(2,1)S(1)} %dynamic_update_slice.26, bf16[128,12,48]{1,2,0:T(8,128)(2,1)S(1)} %copy.115, s32[]{:T(128)} %constant.81.clone.1, s32[]{:T(128)S(6)} %select_n.61, s32[]{:T(128)} %constant.81.clone.1) | dynamic-update-slice | bytes 294916 | tf_op jit(solution)/shard_map/dynamic_update_slice | solution.py:17
  137.1 1.9 copy.116
  139.0 28.4 %dynamic_update_slice.28 = bf16[128,96,48]{1,2,0:T(8,128)(2,1)S(1)} dynamic-update-slice(bf16[128,96,48]{1,2,0:T(8,128)(2,1)S(1)} %dynamic_update_slice.27, bf16[128,12,48]{1,2,0:T(8,128)(2,1)S(1)} %copy.116, s32[]{:T(128)} %constant.81.clone.1, s32[]{:T(128)S(6)} %select_n.63, s32[]{:T(128)} %constant.81.clone.1) | dynamic-update-slice | bytes 294916 | tf_op jit(solution)/shard_map/dynamic_update_slice | solution.py:22
  167.4 1.9 copy.117
  169.3 28.4 %dynamic_update_slice.29 = bf16[128,96,48]{1,2,0:T(8,128)(2,1)S(1)} dynamic-update-slice(bf16[128,96,48]{1,2,0:T(8,128)(2,1)S(1)} %dynamic_update_slice.28, bf16[128,12,48]{1,2,0:T(8,128)(2,1)S(1)} %copy.117, s32[]{:T(128)} %constant.81.clone.1, s32[]{:T(128)S(6)} %select_n.65, s32[]{:T(128)} %constant.81.clone.1) | dynamic-update-slice | bytes 294916 | tf_op jit(solution)/shard_map/dynamic_update_slice | solution.py:17
  197.7 1.9 copy.118
  199.6 28.4 %dynamic_update_slice.30 = bf16[128,96,48]{1,2,0:T(8,128)(2,1)S(1)} dynamic-update-slice(bf16[128,96,48]{1,2,0:T(8,128)(2,1)S(1)} %dynamic_update_slice.29, bf16[128,12,48]{1,2,0:T(8,128)(2,1)S(1)} %copy.118, s32[]{:T(128)} %constant.81.clone.1, s32[]{:T(128)S(6)} %select_n.67, s32[]{:T(128)} %constant.81.clone.1) | dynamic-update-slice | bytes 294916 | tf_op jit(solution)/shard_map/dynamic_update_slice | solution.py:22
  228.0 1.9 copy.119
  230.0 28.6 %dynamic_update_slice.31 = bf16[128,96,48]{1,2,0:T(8,128)(2,1)S(1)} dynamic-update-slice(bf16[128,96,48]{1,2,0:T(8,128)(2,1)S(1)} %dynamic_update_slice.30, bf16[128,12,48]{1,2,0:T(8,128)(2,1)S(1)} %copy.119, s32[]{:T(128)} %constant.81.clone.1, s32[]{:T(128)S(6)} %select_n.69, s32[]{:T(128)} %constant.81.clone.1) | dynamic-update-slice | bytes 294916 | tf_op jit(solution)/shard_map/dynamic_update_slice | solution.py:17
  258.6 1.6 fusion.76
  260.2 1.5 copy.121
  262.2 19.1 %reduce-scatter.2.cloned.1.call-done = f32[128,12,48]{0,1,2:T(8,128)} async-done(((f32[128,12,96]{0,1,2:T(8,128)}), f32[128,12,48]{0,1,2:T(8,128)}) %reduce-scatter.2.cloned.1.call-update) | async-done | bytes 294928 | tf_op jit(solution)/shard_map/reduce_scatter | solution.py:80
  281.3 1.2 reduce_sum.92
  282.7 1.3 multiply_reduce_fusion.1
  284.2 1.3 multiply_convert_fusion.1
  286.1 0.4 convolution_bitcast_fusion
  286.5 0.9 fusion.24
  287.3 6.1 %all_gather.6 = bf16[128,12,96]{0,2,1:T(8,128)(2,1)S(1)} all-gather(bf16[128,12,48]{0,2,1:T(8,128)(2,1)S(1)} %get-tuple-element.6), channel_id=1, replica_groups=mesh['grp'=2,'row'=8,'col'=2] {'col'}, dimensions={2}, use_global_device_ids=true | all-gather | bytes 442368 | tf_op jit(solution)/shard_map/all_gather | solution.py:83
  293.4 0.9 copy.130
  294.3 4.6 %all-to-all-start = ((bf16[128,12,96]{0,1,2:T(8,128)(2,1)}), bf16[128,12,96]{0,1,2:T(8,128)(2,1)S(1)}, u32[]{:S(2)}, u32[]{:S(2)}) async-start(bf16[128,12,96]{0,1,2:T(8,128)(2,1)} %copy.130), calls=%async_computation.1 | async-start | bytes 786432 | tf_op jit(solution)/shard_map/all_to_all | solution.py:84
  298.9 1.1 fusion.8
  300.0 17.1 %all-to-all-done = bf16[128,12,96]{0,1,2:T(8,128)(2,1)S(1)} async-done(((bf16[128,12,96]{0,1,2:T(8,128)(2,1)}), bf16[128,12,96]{0,1,2:T(8,128)(2,1)S(1)}, u32[]{:S(2)}, u32[]{:S(2)}) %all-to-all-start) | async-done | bytes 294944 | tf_op jit(solution)/shard_map/all_to_all | solution.py:84
  317.2 1.2 copy.133
  318.4 5.3 %copy.134 = bf16[128,96,48]{2,1,0:T(8,128)(2,1)S(1)} copy(bf16[128,96,48]{0,2,1:T(8,128)(2,1)} %all-gather.2.cloned.1.call-done) | data formatting | bytes 2359296 | tf_op jit(solution)/shard_map/all_gather | solution.py:86
  323.7 2.0 fusion.74
  326.1 0.6 copy-done.2
  326.8 0.4 fusion.75
  327.5 0.5 fusion.53
  328.1 1.1 fusion.14
  (66 shorter events, 3.0 us)
Async XLA Ops:
  6.5 320.9 %copy-start = (bf16[128,1024]{1,0:T(8,128)(2,1)S(1)}, bf16[128,1024]{1,0:T(8,128)(2,1)}, u32[]{:S(2)}) copy-start(bf16[128,1024]{1,0:T(8,128)(2,1)} %param.12) | copy-start | bytes 786436
  6.5 274.8 %reduce-scatter.2.cloned.1.call-start = ((), (), s32[]{:S(2)}) async-start(), calls=%async_computation.2 | async-start | bytes 1179648 | tf_op jit(solution)/shard_map/reduce_scatter | solution.py:80
  9.5 2.7 copy-start.9
  12.2 7.5 %collective-permute-start = (bf16[128,12,48]{0,2,1:T(8,128)(2,1)S(1)}, bf16[128,12,48]{0,2,1:T(8,128)(2,1)S(1)}, u32[]{:S(2)}, u32[]{:S(2)}) collective-permute-start(bf16[128,12,48]{0,2,1:T(8,128)(2,1)S(1)} %get-tuple-element.7), channel_id=1, source_target_pairs={{0,2},{2,4},{4,6},{6,8},{8,10},{10,12},{12,14},{14,0},{1,3},{3,5},... | collective-permute-start | bytes 442376 | tf_op jit(solution)/shard_map/ppermute | solution.py:16
  12.8 7.0 %collective-permute-start.1 = (bf16[128,12,48]{0,2,1:T(8,128)(2,1)S(1)}, bf16[128,12,48]{0,2,1:T(8,128)(2,1)S(1)}, u32[]{:S(2)}, u32[]{:S(2)}) collective-permute-start(bf16[128,12,48]{0,2,1:T(8,128)(2,1)S(1)} %get-tuple-element.7), channel_id=1, source_target_pairs={{0,14},{2,0},{4,2},{6,4},{8,6},{10,8},{12,10},{14,12},{1,15},{3,1}... | collective-permute-start | bytes 442376 | tf_op jit(solution)/shard_map/ppermute | solution.py:21
  19.7 16.8 %copy-start.7 = (bf16[128,12,48]{0,2,1:T(8,128)(2,1)}, bf16[128,12,48]{0,2,1:T(8,128)(2,1)S(1)}, u32[]{:S(2)}) copy-start(bf16[128,12,48]{0,2,1:T(8,128)(2,1)S(1)} %collective-permute-done) | copy-start | bytes 442372
  19.7 7.2 %collective-permute-start.2 = (bf16[128,12,48]{0,2,1:T(8,128)(2,1)S(1)}, bf16[128,12,48]{0,2,1:T(8,128)(2,1)S(1)}, u32[]{:S(2)}, u32[]{:S(2)}) collective-permute-start(bf16[128,12,48]{0,2,1:T(8,128)(2,1)S(1)} %collective-permute-done), channel_id=1, source_target_pairs={{0,2},{2,4},{4,6},{6,8},{8,10},{10,12},{12,14},{14,0},{1,3},{3,5},... | collective-permute-start | bytes 442376 | tf_op jit(solution)/shard_map/ppermute | solution.py:16
  19.7 16.8 %copy-start.5 = (bf16[128,12,48]{0,2,1:T(8,128)(2,1)}, bf16[128,12,48]{0,2,1:T(8,128)(2,1)S(1)}, u32[]{:S(2)}) copy-start(bf16[128,12,48]{0,2,1:T(8,128)(2,1)S(1)} %collective-permute-done.1) | copy-start | bytes 442372
  19.8 7.2 %collective-permute-start.3 = (bf16[128,12,48]{0,2,1:T(8,128)(2,1)S(1)}, bf16[128,12,48]{0,2,1:T(8,128)(2,1)}, u32[]{:S(2)}, u32[]{:S(2)}) collective-permute-start(bf16[128,12,48]{0,2,1:T(8,128)(2,1)S(1)} %collective-permute-done.1), channel_id=1, source_target_pairs={{0,14},{2,0},{4,2},{6,4},{8,6},{10,8},{12,10},{14,12},{1,15},{3,1}... | collective-permute-start | bytes 442376 | tf_op jit(solution)/shard_map/ppermute | solution.py:21
  27.0 9.6 %copy-start.6 = (bf16[128,12,48]{0,2,1:T(8,128)(2,1)}, bf16[128,12,48]{0,2,1:T(8,128)(2,1)S(1)}, u32[]{:S(2)}) copy-start(bf16[128,12,48]{0,2,1:T(8,128)(2,1)S(1)} %collective-permute-done.2) | copy-start | bytes 442372
  27.0 7.3 %collective-permute-start.4 = (bf16[128,12,48]{0,2,1:T(8,128)(2,1)S(1)}, bf16[128,12,48]{0,2,1:T(8,128)(2,1)}, u32[]{:S(2)}, u32[]{:S(2)}) collective-permute-start(bf16[128,12,48]{0,2,1:T(8,128)(2,1)S(1)} %collective-permute-done.2), channel_id=1, source_target_pairs={{0,2},{2,4},{4,6},{6,8},{8,10},{10,12},{12,14},{14,0},{1,3},{3,5},... | collective-permute-start | bytes 442376 | tf_op jit(solution)/shard_map/ppermute | solution.py:16
  27.0 170.7 %collective-permute-start.5 = (bf16[128,12,48]{0,2,1:T(8,128)(2,1)}, bf16[128,12,48]{0,2,1:T(8,128)(2,1)}, u32[]{:S(2)}, u32[]{:S(2)}) collective-permute-start(bf16[128,12,48]{0,2,1:T(8,128)(2,1)} %collective-permute-done.3), channel_id=1, source_target_pairs={{0,14},{2,0},{4,2},{6,4},{8,6},{10,8},{12,10},{14,12},{1,15},{3,1}... | collective-permute-start | bytes 442376 | tf_op jit(solution)/shard_map/ppermute | solution.py:21
  34.3 193.8 %collective-permute-start.6 = (bf16[128,12,48]{0,2,1:T(8,128)(2,1)}, bf16[128,12,48]{0,2,1:T(8,128)(2,1)}, u32[]{:S(2)}, u32[]{:S(2)}) collective-permute-start(bf16[128,12,48]{0,2,1:T(8,128)(2,1)} %collective-permute-done.4), channel_id=1, source_target_pairs={{0,2},{2,4},{4,6},{6,8},{8,10},{10,12},{12,14},{14,0},{1,3},{3,5},... | collective-permute-start | bytes 442376 | tf_op jit(solution)/shard_map/ppermute | solution.py:16
  260.1 1.7 copy-start.3
  260.1 1.7 copy-start.10
  260.1 1.7 copy-start.12
  261.6 56.8 %all-gather.2.cloned.1.call-start = ((), (), s32[]{:S(2)}) async-start(), calls=%async_computation.3 | async-start | bytes 1327104 | tf_op jit(solution)/shard_map/all_gather | solution.py:86
  261.9 23.6 %copy-start.8 = (bf16[2,128,128]{2,1,0:T(8,128)(2,1)S(1)}, bf16[2,128,128]{2,1,0:T(8,128)(2,1)}, u32[]{:S(2)}) copy-start(bf16[2,128,128]{2,1,0:T(8,128)(2,1)} %param.11) | copy-start | bytes 196612
  285.8 13.2 %copy-start.1 = (f32[12,48,128]{2,1,0:T(8,128)}, f32[12,48,128]{2,1,0:T(8,128)S(1)}, u32[]{:S(2)}) copy-start(f32[12,48,128]{2,1,0:T(8,128)S(1)} %get-tuple-element.12) | copy-start | bytes 884740
  294.3 22.8 %all-to-all-start = ((bf16[128,12,96]{0,1,2:T(8,128)(2,1)}), bf16[128,12,96]{0,1,2:T(8,128)(2,1)S(1)}, u32[]{:S(2)}, u32[]{:S(2)}) async-start(bf16[128,12,96]{0,1,2:T(8,128)(2,1)} %copy.130), calls=%async_computation.1 | async-start | bytes 786432 | tf_op jit(solution)/shard_map/all_to_all | solution.py:84
  325.7 1.0 copy-start.2
  325.7 1.0 copy-start.4
  327.2 0.9 copy-start.11
Sparse Core Ops, SparseCore 0:
  261.8 19.5 reduce-scatter.1
  287.5 30.0 all-gather.1
